TPU v7x, 512 devices: a whole 4x8x8 slice. The times are simulated.
512 devices in a mesh: claims: 16 (over y, core), feat: 32 (over z, x).
Axes of the slice: x: 4, y: 8, z: 8, core: 2. Of those that a mesh axis runs over, the one named last changes fastest.
Arguments:
- design: bfloat16 [32768, 16384], P('claims', 'feat'), may hold values from -0.09375 to 0.09375
- irls_weights: float32 [32768], P('claims'), may hold values from 0.2 to 5
- ridge_diag: float32 [16384], P('feat'), may hold values from 0.5 to 2
- gradients: float32 [16384, 8], P('feat'), may hold values from -45 to 45
Outputs:
- solution: float32 [16384, 8], P('feat')
- residual: float32 [16384, 8], P('feat')
All inputs are finite; a program needn't handle non-finite values.
Results may differ from a plain program's by a relative error of at most 0.0085.
Values may be sent and summed in bfloat16 or wider, within the bound.
A program may use at most 64 MiB of HBM per device.

v0:
```python
import jax
import jax.numpy as jnp
from jax import lax
from jax.sharding import PartitionSpec as P

ITERS = 2


def shards(design, irls_weights, ridge_diag, gradients):
    rows_local, width_local = design.shape
    claim_count = lax.axis_size("claims")
    feat_share = width_local // claim_count
    own_offset = lax.axis_index("claims") * feat_share

    def own_slice(values):
        return lax.dynamic_slice_in_dim(values, own_offset, feat_share, 0)

    def own_view(values):
        return own_slice(values)

    residual = gradients
    direction = residual
    solution = jnp.zeros_like(residual)
    own_res = own_view(residual)
    norm_now = lax.psum(jnp.sum(own_res * own_res, axis=0), ("claims", "feat"))
    dir_half = gradients.astype(jnp.bfloat16)
    for loop_step in range(ITERS):
        partial_rows = jnp.dot(design, dir_half, preferred_element_type=jnp.float32)
        summed = lax.psum(partial_rows, "feat")
        scaled_rows = (irls_weights[:, None] * summed).astype(jnp.bfloat16)
        partial_cols = lax.dot_general(
            design, scaled_rows, (((0,), (0,)), ((), ())), preferred_element_type=jnp.float32
        )
        hess_image = lax.psum(partial_cols, "claims") + ridge_diag[:, None] * direction
        own_dir = own_view(direction)
        own_image = own_view(hess_image)
        curvature = lax.psum(jnp.sum(own_dir * own_image, axis=0), ("claims", "feat"))
        step_size = norm_now / curvature
        solution = solution + step_size * direction
        residual = residual - step_size * hess_image
        if loop_step + 1 < ITERS:
            own_res = own_view(residual)
            norm_next = lax.psum(jnp.sum(own_res * own_res, axis=0), ("claims", "feat"))
        if loop_step + 1 < ITERS:
            direction = residual + norm_next / norm_now * direction
            norm_now = norm_next
            dir_half = direction.astype(jnp.bfloat16)
    return (solution, residual)


def solution(mesh):
    in_specs = (P("claims", "feat"), P("claims"), P("feat"), P("feat", None))
    out_specs = (P("feat", None), P("feat", None))
    return jax.shard_map(shards, mesh=mesh, in_specs=in_specs, out_specs=out_specs, check_vma=False)
```

profile of v0, /device:TPU:1, one launch (start us, length us, event | category | flops | bytes accessed | tf_op | source)
XLA Modules:
  0.0 724.9 jit_solution(13984271514909632763)
XLA Ops:
  7.2 0.0 copy-start
  7.2 0.0 copy-start.2
  7.2 0.0 all-reduce.4.cloned.1.call-start
  7.2 1.5 copy-done
  8.8 2.4 fusion.3
  11.2 0.0 copy-start.1
  11.2 0.0 copy-start.3
  11.2 0.0 all-reduce.4.cloned.1.call-update
  11.2 0.0 all-reduce.6.cloned.1.call-start
  11.3 162.1 %all-reduce.4.cloned.1.call-done = f32[2048,8]{1,0:T(8,128)} async-done(((f32[2048,8]{1,0:T(8,128)}), f32[2048,8]{1,0:T(8,128)}) %all-reduce.4.cloned.1.call-update) | async-done | bytes 65552 | tf_op jit(solution)/shard_map/psum | solution.py:29
  173.4 0.0 copy-done.2
  173.4 2.0 convolution_bitcast_fusion.2
  175.4 47.4 %psum.58 = f32[512,8]{0,1:T(8,128)S(1)} all-reduce(f32[512,8]{0,1:T(8,128)S(1)} %convolution_bitcast_fusion.2), channel_id=1, replica_groups=mesh['claims'=16,'feat'=32] {'claims'}, use_global_device_ids=true, to_apply=%region_3.0 | all-reduce | flops 4096 | bytes 32768 | tf_op jit(solution)/shard_map/psum | solution.py:34
  222.8 0.0 copy-done.1
  222.8 0.0 copy-done.3
  222.8 0.2 multiply_reduce_fusion.2
  223.0 98.1 %all-reduce = (f32[8]{0:T(128)S(1)}, f32[8]{0:T(128)S(1)}) all-reduce(f32[8]{0:T(128)S(1)} %get-tuple-element.3, f32[8]{0:T(128)S(1)} %get-tuple-element.2), channel_id=1, replica_groups=mesh['claims'=16,'feat'=32] {'claims','feat'}, use_global_device_ids=true, to_apply=%region_1.0 | all-reduce | flops 16 | bytes 128 | tf_op jit(solution)/shard_map/psum | solution.py:25
  321.1 0.1 multiply_subtract_fusion.1
  321.2 0.2 multiply_reduce_fusion.1
  321.4 95.0 %psum.60 = f32[8]{0:T(128)S(1)} all-reduce(f32[8]{0:T(128)S(1)} %multiply_reduce_fusion.1), channel_id=1, replica_groups=mesh['claims'=16,'feat'=32] {'claims','feat'}, use_global_device_ids=true, to_apply=%region_7.0 | all-reduce | flops 8 | bytes 64 | tf_op jit(solution)/shard_map/psum | solution.py:43
  416.4 0.1 multiply_add_fusion.2
  416.5 1.7 convolution_bitcast_fusion
  418.2 0.0 all-reduce.6.cloned.1.call-update
  418.2 151.5 %all-reduce.6.cloned.1.call-done = f32[2048,8]{1,0:T(8,128)} async-done(((f32[2048,8]{1,0:T(8,128)}), f32[2048,8]{1,0:T(8,128)}) %all-reduce.6.cloned.1.call-update) | async-done | bytes 65552 | tf_op jit(solution)/shard_map/psum | solution.py:29
  569.7 2.0 convolution_bitcast_fusion.1
  571.7 47.4 %psum.62 = f32[512,8]{0,1:T(8,128)S(1)} all-reduce(f32[512,8]{0,1:T(8,128)S(1)} %convolution_bitcast_fusion.1), channel_id=1, replica_groups=mesh['claims'=16,'feat'=32] {'claims'}, use_global_device_ids=true, to_apply=%region_9.0 | all-reduce | flops 4096 | bytes 32768 | tf_op jit(solution)/shard_map/psum | solution.py:34
  619.1 0.2 multiply_reduce_fusion
  619.3 98.1 %psum.63 = f32[8]{0:T(128)S(1)} all-reduce(f32[8]{0:T(128)S(1)} %multiply_reduce_fusion), channel_id=1, replica_groups=mesh['claims'=16,'feat'=32] {'claims','feat'}, use_global_device_ids=true, to_apply=%region_11.0 | all-reduce | flops 8 | bytes 64 | tf_op jit(solution)/shard_map/psum | solution.py:37
  717.4 0.7 multiply_subtract_fusion
  (5 shorter events, 0.0 us)
Async XLA Ops:
  7.2 1.6 copy-start
  7.2 166.2 %copy-start.2 = (f32[2048]{0:T(1024)S(1)}, f32[2048]{0:T(1024)}, u32[]{:S(2)}) copy-start(f32[2048]{0:T(1024)} %param.5) | copy-start | bytes 24580
  7.2 166.2 %all-reduce.4.cloned.1.call-start = ((), (), s32[]{:S(2)}) async-start(), calls=%async_computation | async-start | bytes 2097152 | tf_op jit(solution)/shard_map/psum | solution.py:29
  11.2 211.6 %copy-start.1 = (f32[512,8]{0,1:T(8,128)S(1)}, f32[512,8]{0,1:T(8,128)}, u32[]{:S(2)}) copy-start(f32[512,8]{0,1:T(8,128)} %param.7) | copy-start | bytes 49156
  11.2 211.6 %copy-start.3 = (f32[512]{0:T(512)S(1)}, f32[512]{0:T(512)}, u32[]{:S(2)}) copy-start(f32[512]{0:T(512)} %param.6) | copy-start | bytes 6148
  11.2 558.5 %all-reduce.6.cloned.1.call-start = ((), (), s32[]{:S(2)}) async-start(), calls=%async_computation.1 | async-start | bytes 2097152 | tf_op jit(solution)/shard_map/psum | solution.py:29
Sparse Core Ops, SparseCore 0:
  11.5 161.8 all-reduce.3
  418.3 151.3 all-reduce.5
where the time goes:
time: 725 us
  blocking collectives  386 us (53%)
  waiting for transfers between devices  314 us (43%)
  between operations  14.1 us (2%)
  matrix products  8.1 us (1%)
    psum x2, waiting for transfers between devices, shards(): summed = lax.psum(partial_rows, 'feat')  314 us
    psum x1, blocking collectives, shards(): lax.psum(jnp.sum(own_dir * own_image, axis=0), ('claims', 'feat'))  98.1 us
    psum x1, blocking collectives, shards(): norm_now = lax.psum(jnp.sum(own_res * own_res, axis=0), ('claims', 'feat'))  98.1 us
    psum x1, blocking collectives, shards(): norm_next = lax.psum(jnp.sum(own_res * own_res, axis=0), ('claims', 'feat'))  95 us
    psum x2, blocking collectives, shards(): lax.psum(partial_cols, 'claims') + ridge_diag[:, None] * direction  94.8 us
  transfers between devices with their start and end apart: 2, of which 2 were waited for; matrix products, arithmetic and copies ran while one was open for 0% of the time, Pallas kernels for 0%

commit v1 on v0

v1 whole, which is shorter than its diff:
```python
import functools

import jax
import jax.numpy as jnp
from jax import lax
from jax.experimental import pallas as pl
from jax.experimental.pallas import tpu as pltpu
from jax.sharding import PartitionSpec as P

MESH = pl.DeviceIdType.MESH
BF16, F32 = jnp.bfloat16, jnp.float32
NX, NZ, NY = 4, 8, 8
K = 8
ROWS_LOCAL, WIDTH = 2048, 512
SEG = ROWS_LOCAL // 4
HALF = WIDTH // 2
ZS = (4, 3, 5, 2, 6, 1, 7)
NT = (((1,), (1,)), ((), ()))


def kernel(
    x_hbm, w_hbm, rd_hbm, g_hbm, sol_ref, res_ref,
    xv, wv, rdv, gv, y_opp, y_in, z_in, h_in, s_in,
    q_src, qz_in, qx_in, qy_in, qc_in,
    load_sem, xsem, send_sem, recv_sem,
):
    c, f = lax.axis_index("claims"), lax.axis_index("feat")
    y, core = c // 2, lax.rem(c, 2)
    z, x = f // NX, lax.rem(f, NX)
    par = lax.rem(z, 2)
    opp = 1 - par
    slot = par * NX + x
    z_pair = z + 1 - 2 * par
    c_pair = c + 1 - 2 * core

    loads = [
        pltpu.make_async_copy(src, dst, load_sem.at[i])
        for i, (src, dst) in enumerate(((g_hbm, gv), (rd_hbm, rdv), (w_hbm, wv)))
    ]
    loads[0].start()

    def x_load(seg):
        rows = pl.ds(pl.multiple_of(seg * SEG, SEG), SEG)
        return pltpu.make_async_copy(x_hbm.at[rows], xv.at[rows], xsem.at[seg])

    seg_order = (2 * par, 2 * par + 1, 2 * opp, 2 * opp + 1)
    for seg in seg_order:
        x_load(seg).start()
    loads[1].start()
    loads[2].start()

    barrier = pltpu.get_barrier_semaphore()
    z_peers = [lax.rem(z + k, NZ) * NX + x for k in ZS]
    x_peers = [z * NX + lax.rem(x + k, NX) for k in (2, 1, 3)]
    d_peers = [z_pair * NX + lax.rem(x + k, NX) for k in (2, 1, 3, 0)]
    y_peers = [lax.rem(y + k, NY) * 2 + core for k in ZS]
    for peer in z_peers + x_peers + d_peers[:3]:
        pl.semaphore_signal(barrier, 1, device_id={"feat": peer}, device_id_type=MESH)
    for peer in y_peers + [c_pair]:
        pl.semaphore_signal(barrier, 1, device_id={"claims": peer}, device_id_type=MESH)

    lane = lax.broadcasted_iota(jnp.int32, (K, 128), 1)
    sub = lax.broadcasted_iota(jnp.int32, (K, 128), 0)

    def to_row(*columns):
        tile = jnp.zeros((K, 128), F32)
        for j, column in enumerate(columns):
            tile = jnp.where(lane == sub + K * j, column, tile)
        return jnp.sum(tile, axis=0, keepdims=True)

    def from_row(row, j):
        return jnp.sum(jnp.where(lane == sub + K * j, row, 0.0), axis=1, keepdims=True)

    def send(src, dst, it, kind, device):
        pltpu.make_async_remote_copy(
            src, dst, send_sem.at[it, kind], recv_sem.at[it, kind],
            device_id=device, device_id_type=MESH,
        ).start()

    def arrived(ref, it, kind):
        pltpu.make_async_copy(ref, ref, recv_sem.at[it, kind]).wait()

    def row_seg(seg):
        return pl.ds(pl.multiple_of(seg * SEG, SEG), SEG)

    def feat_sum(it, product, columns):
        for own, half in ((True, par), (False, opp)):
            block = jnp.concatenate([product(2 * half), product(2 * half + 1)], axis=0).astype(BF16)
            if own:
                y_in[it, z] = block
                if it == 0:
                    pl.semaphore_wait(barrier, 21)
            else:
                y_opp[it] = block
            for k, peer in zip(ZS, z_peers):
                if (k % 2 == 0) == own:
                    send(y_in.at[it, z] if own else y_opp.at[it], y_in.at[it, z], it, 0, {"feat": peer})
        qz_in[it, z] = to_row(*columns)
        for peer in z_peers:
            send(qz_in.at[it, z], qz_in.at[it, z], it, 1, {"feat": peer})
        arrived(y_in.at[it, pl.ds(0, NZ - 1)], it, 0)
        total = y_in[it, 0].astype(F32)
        for j in range(1, NZ):
            total += y_in[it, j].astype(F32)
        z_in[it, slot] = total.astype(BF16)
        for near, far in zip(x_peers, d_peers):
            send(z_in.at[it, slot], z_in.at[it, slot], it, 2, {"feat": far})
            send(z_in.at[it, slot], z_in.at[it, slot], it, 2, {"feat": near})
        send(z_in.at[it, slot], z_in.at[it, slot], it, 2, {"feat": d_peers[3]})
        arrived(qz_in.at[it, pl.ds(0, NZ - 1)], it, 1)
        qx_in[it, x] = jnp.sum(qz_in[it], axis=0)
        for peer in x_peers:
            send(qx_in.at[it, x], qx_in.at[it, x], it, 3, {"feat": peer})
        arrived(qx_in.at[it, pl.ds(0, NX - 1)], it, 3)
        row = jnp.sum(qx_in[it], axis=0)
        arrived(z_in.at[it, pl.ds(0, 2 * NX - 1)], it, 2)
        halves = []
        for half in range(2):
            total = z_in[it, half * NX].astype(F32)
            for j in range(1, NX):
                total += z_in[it, half * NX + j].astype(F32)
            halves.append(total)
        return halves, row

    def claims_sum(it, halves):
        image = jnp.zeros((K, WIDTH), F32)
        energy = jnp.zeros((K, SEG), F32)
        for half in range(2):
            for s in range(2):
                seg = 2 * half + s
                values = halves[half][K * s:K * (s + 1)]
                weighted = wv[:, seg * SEG:(seg + 1) * SEG] * values
                energy += weighted * values
                image += jnp.dot(weighted.astype(BF16), xv[seg * SEG:(seg + 1) * SEG, :],
                                 preferred_element_type=F32)
        h_in[it, y] = jnp.concatenate([image[:, :HALF], image[:, HALF:]], axis=0).astype(BF16)
        for peer in y_peers:
            send(h_in.at[it, y], h_in.at[it, y], it, 4, {"claims": peer})
        qy_in[it, y] = to_row(jnp.sum(energy, axis=1, keepdims=True))
        for peer in y_peers:
            send(qy_in.at[it, y], qy_in.at[it, y], it, 5, {"claims": peer})
        arrived(h_in.at[it, pl.ds(0, NY - 1)], it, 4)
        total = h_in[it, 0].astype(F32)
        for j in range(1, NY):
            total += h_in[it, j].astype(F32)
        s_in[it, core] = total
        send(s_in.at[it, core], s_in.at[it, core], it, 6, {"claims": c_pair})
        arrived(qy_in.at[it, pl.ds(0, NY - 1)], it, 5)
        qc_in[it, core] = jnp.sum(qy_in[it], axis=0)
        send(qc_in.at[it, core], qc_in.at[it, core], it, 7, {"claims": c_pair})
        arrived(s_in.at[it, 0], it, 6)
        both = s_in[it, 0] + s_in[it, 1]
        image = jnp.concatenate([both[:K], both[K:]], axis=1)
        arrived(qc_in.at[it, 0], it, 7)
        return image, from_row(qc_in[it, 0] + qc_in[it, 1], 0)

    loads[0].wait()
    grad = gv[...]
    grad_half = grad.astype(BF16)

    def first_product(seg):
        x_load(seg).wait()
        return lax.dot_general(grad_half, xv[row_seg(seg), :], NT, preferred_element_type=F32)

    loads[1].wait()
    ridge = rdv[...]
    ridge_grad = ridge * grad
    halves, row = feat_sum(
        0, first_product,
        (jnp.sum(grad * grad, axis=1, keepdims=True), jnp.sum(ridge_grad * grad, axis=1, keepdims=True)),
    )
    loads[2].wait()
    image, energy = claims_sum(0, halves)
    norm_now, ridge_gg = from_row(row, 0), from_row(row, 1)
    step_one = norm_now / (energy + ridge_gg)
    residual = grad - step_one * (image + ridge_grad)

    high = residual.astype(BF16).astype(F32)
    pair = jnp.concatenate([high, residual - high], axis=0).astype(BF16)

    def second_product(seg):
        both = lax.dot_general(pair, xv[row_seg(seg), :], NT, preferred_element_type=F32)
        return both[:K] + both[K:]

    ridge_res = ridge * residual
    res_halves, row = feat_sum(
        1, second_product,
        (
            jnp.sum(residual * residual, axis=1, keepdims=True),
            jnp.sum(ridge_res * residual, axis=1, keepdims=True),
            jnp.sum(ridge_res * grad, axis=1, keepdims=True),
        ),
    )
    norm_next = from_row(row, 0)
    beta = norm_next / norm_now
    beta_two = jnp.concatenate([beta, beta], axis=0)
    image, energy = claims_sum(1, [r + beta_two * h for r, h in zip(res_halves, halves)])
    ridge_dd = from_row(row, 1) + beta * (2.0 * from_row(row, 2) + beta * ridge_gg)
    step_two = norm_next / (energy + ridge_dd)
    direction = residual + beta * grad
    sol_ref[...] = step_one * grad + step_two * direction
    res_ref[...] = residual - step_two * (image + ridge * direction)

    for it in range(2):
        for kind, ref in (
            (0, y_in.at[it, pl.ds(0, NZ - 1)]),
            (1, qz_in.at[it, pl.ds(0, NZ - 1)]),
            (2, z_in.at[it, pl.ds(0, 2 * NX - 1)]),
            (3, qx_in.at[it, pl.ds(0, NX - 1)]),
            (4, h_in.at[it, pl.ds(0, NY - 1)]),
            (5, qy_in.at[it, pl.ds(0, NY - 1)]),
            (6, s_in.at[it, 0]),
            (7, qc_in.at[it, 0]),
        ):
            pltpu.make_async_copy(ref, ref, send_sem.at[it, kind]).wait()


def shards(design, irls_weights, ridge_diag, gradients):
    hbm = pl.BlockSpec(memory_space=pltpu.HBM)
    vmem = pl.BlockSpec(memory_space=pltpu.VMEM)
    sol, res = pl.pallas_call(
        kernel,
        out_shape=[jax.ShapeDtypeStruct((K, WIDTH), F32)] * 2,
        in_specs=[hbm] * 4,
        out_specs=[vmem] * 2,
        scratch_shapes=[
            pltpu.VMEM((ROWS_LOCAL, WIDTH), BF16),
            pltpu.VMEM((1, ROWS_LOCAL), F32),
            pltpu.VMEM((1, WIDTH), F32),
            pltpu.VMEM((K, WIDTH), F32),
            pltpu.VMEM((2, 2 * K, SEG), BF16),
            pltpu.VMEM((2, NZ, 2 * K, SEG), BF16),
            pltpu.VMEM((2, 2 * NX, 2 * K, SEG), BF16),
            pltpu.VMEM((2, NY, 2 * K, HALF), BF16),
            pltpu.VMEM((2, 2, 2 * K, HALF), F32),
            pltpu.VMEM((1, 128), F32),
            pltpu.VMEM((2, NZ, 1, 128), F32),
            pltpu.VMEM((2, NX, 1, 128), F32),
            pltpu.VMEM((2, NY, 1, 128), F32),
            pltpu.VMEM((2, 2, 1, 128), F32),
            pltpu.SemaphoreType.DMA((3,)),
            pltpu.SemaphoreType.DMA((4,)),
            pltpu.SemaphoreType.DMA((2, 8)),
            pltpu.SemaphoreType.DMA((2, 8)),
        ],
        compiler_params=pltpu.CompilerParams(collective_id=0, has_side_effects=True),
        name="cg",
    )(design, irls_weights.reshape(1, ROWS_LOCAL), ridge_diag.reshape(1, WIDTH), gradients.T)
    return sol.T, res.T


def solution(mesh):
    in_specs = (P("claims", "feat"), P("claims"), P("feat"), P("feat", None))
    out_specs = (P("feat", None), P("feat", None))
    return jax.shard_map(shards, mesh=mesh, in_specs=in_specs, out_specs=out_specs, check_vma=False)
```

time: 725 us -> 51.9 us (0.07)
  blocking collectives: 386 us -> 0 us
  waiting for transfers between devices: 314 us -> 0 us
  Pallas kernels: 0 us -> 48.3 us
  between operations: 14.1 us -> 0.64 us
  matrix products: 8.1 us -> 0 us
    psum x5 -> x0, blocking collectives: 386 us -> none  [the longest x1 98.1 us: shards(): lax.psum(jnp.sum(own_dir * own_image, axis=0), ('claims', 'feat'))]
    psum x2 -> x0, waiting for transfers between devices: 314 us -> none  [shards(): summed = lax.psum(partial_rows, 'feat')]
    pallas_call x0 -> x1, Pallas kernels: none -> 48.3 us  [shards(): pl.pallas_call(kernel, out_shape=[jax.ShapeDtypeStruct((K, WIDTH), F32)]...]
    dot_general x4 -> x0, matrix products: 8.1 us -> none  [the longest x2 4.15 us: shards(): partial_rows = jnp.dot(design, dir_half, preferred_element_type=jnp.float32)]
  transfers between devices with their start and end apart: 2 -> 0, of which waited for: 2 -> 0; matrix products, arithmetic and copies ran while one was open for 0% -> 0% of each run, Pallas kernels for 0% -> 0%
where the time goes in v1:
time: 51.9 us; the launch traced here: 51.6 us
  Pallas kernels  48.3 us (93%)
  local copies, waits for them, and re-layouts  2.65 us (5%)
  between operations  0.64 us (1%)
    pallas_call x1, Pallas kernels, shards(): pl.pallas_call(kernel, out_shape=[jax.ShapeDtypeStruct((K, WIDTH), F32)]...  48.3 us
    unnamed x2, local copies, waits for them, and re-layouts  2.65 us

profile of v1, /device:TPU:1, one launch (start us, length us, event | category | flops | bytes accessed | tf_op | source)
XLA Modules:
  0.0 51.6 jit_solution(173377426032531560)
XLA Ops:
  0.6 48.3 %cg.1 = (f32[8,512]{1,0:T(8,128)}, f32[8,512]{1,0:T(8,128)}) custom-call(bf16[2048,512]{1,0:T(8,128)(2,1)} %x_hbm.1, f32[1,2048]{1,0:T(1,128)} %bitcast.8, f32[1,512]{1,0:T(1,128)} %bitcast.9, f32[8,512]{1,0:T(8,128)} %bitcast.5), custom_call_target="tpu_custom_call" | custom-call | tf_op jit(solution)/shard_map/cg/pallas_call | solution.py:221
  48.9 1.3 %copy.8 = f32[512,8]{0,1:T(8,128)} copy(f32[512,8]{0,1:T(8,128)} %bitcast.7) | data formatting | bytes 32768
  50.2 1.3 %copy.9 = f32[512,8]{0,1:T(8,128)} copy(f32[512,8]{0,1:T(8,128)} %bitcast.6) | data formatting | bytes 32768
